TPU v7x, 256 devices: a whole 4x4x8 slice. The times are simulated.
256 devices in a mesh: pb: 16 (over z, core), kv: 16 (over y, x).
Axes of the slice: x: 4, y: 4, z: 8, core: 2. Of those that a mesh axis runs over, the one named last changes fastest.
Arguments:
- queries: bfloat16 [393216, 1024], P(('pb', 'kv')), may hold values from -8 to 8
- keys: bfloat16 [524288, 128], P(('kv', 'pb')), may hold values from -6 to 6
- values: bfloat16 [524288, 128], P(('kv', 'pb')), may hold values from -6 to 6
- selected: int32 [6144, 14], P(('pb', 'kv')), may hold values from 1 to 8190, as said below
Outputs:
- attended: bfloat16 [393216, 1024], P(('pb', 'kv'))
Inputs may be any that keep to these rules, and one draw needn't show every extreme that they name: `selected`: each row names 14 different blocks, never block 0 or block 8191. Key device k holds blocks k * 32 to (k + 1) * 32 - 1, devices counted with kv slowest; query device d holds query blocks d * 24 to (d + 1) * 24 - 1, devices counted with pb slowest. The query blocks of one device name together at most 2 distinct blocks of one key device, and in every draw some key device has exactly 2 named by every query device.
All inputs are finite; a program needn't handle non-finite values.
Results may differ from a plain program's by a relative error of at most 0.0046.
Values may be sent and summed in bfloat16 or wider, within the bound.
A program may use at most 128 MiB of HBM per device.

v0:
```python
import math
import jax
import jax.numpy as jnp
from jax import lax
from jax.sharding import PartitionSpec as P

H = 8
DH = 128
BLOCK = 64
TOPN = 16
QB = 64
CAP = 2


def holdings(wanted, owner, blocks_here):
    local_ids = owner * blocks_here + jnp.arange(blocks_here, dtype=jnp.int32)
    hits = (wanted[:, None] == local_ids[None, :]).astype(jnp.int32)
    present = jnp.max(hits, axis=0)
    return (present, jnp.cumsum(present) - present)


def slot_lists(present, slot_rank, slots):
    local_ids = jnp.arange(present.shape[-1], dtype=jnp.int32)
    slot_ids = jnp.arange(slots, dtype=jnp.int32)
    matches = (present[..., :, None] == 1) & (slot_rank[..., :, None] == slot_ids)
    return jnp.sum(jnp.where(matches, local_ids[:, None], 0), axis=-2)


def per_device(queries, keys, values, selected):
    pb_count = lax.axis_size("pb")
    kv_count = lax.axis_size("kv")
    devices = pb_count * kv_count
    blocks_here = keys.shape[0] // BLOCK
    query_blocks = queries.shape[0] // QB
    column_blocks = pb_count * blocks_here
    tiles_local = jnp.concatenate(
        [keys.reshape(blocks_here, BLOCK, DH), values.reshape(blocks_here, BLOCK, DH)], axis=2
    )
    column = lax.all_gather(tiles_local, "pb", axis=0, tiled=True)
    slots = CAP
    wanted = selected.reshape(-1)
    owners = jnp.arange(devices, dtype=jnp.int32)
    present, slot_rank = jax.vmap(lambda owner: holdings(wanted, owner, blocks_here))(owners)
    owner_lists = slot_lists(present, slot_rank, slots)
    by_column = (
        owner_lists.reshape(kv_count, pb_count, slots)
        + jnp.arange(pb_count, dtype=jnp.int32)[None, :, None] * blocks_here
    )
    by_column = by_column.reshape(kv_count, pb_count * slots)
    asked_for = lax.all_to_all(by_column, "kv", split_axis=0, concat_axis=0, tiled=True)
    outgoing = jnp.take(column, asked_for.reshape(-1), axis=0).reshape(
        kv_count, pb_count * slots, BLOCK, 2 * DH
    )
    fetched = lax.all_to_all(outgoing, "kv", split_axis=0, concat_axis=0, tiled=True)
    tile_table = fetched.reshape(devices * slots, BLOCK, 2 * DH)
    owner_of = selected // blocks_here
    positions = owner_of * slots + jnp.take(slot_rank.reshape(-1), selected)
    me_kv = lax.axis_index("kv")
    ends = jnp.concatenate([column[:1], column[column_blocks - 1 :]], axis=0)
    ends = jnp.where(
        jnp.stack([me_kv == 0, me_kv == kv_count - 1])[:, None, None], ends, jnp.zeros_like(ends)
    )
    ends = lax.psum(ends, "kv")
    tile_table = jnp.concatenate([tile_table, ends], axis=0)
    extra_base = devices * slots
    leading_positions = jnp.broadcast_to(
        jnp.array([extra_base, extra_base + 1], jnp.int32), (query_blocks, 2)
    )
    positions = jnp.concatenate([leading_positions, positions], axis=1)
    group_size = math.gcd(query_blocks, 8)
    q_groups = queries.reshape(query_blocks // group_size, group_size, QB * H, DH)
    p_groups = positions.reshape(query_blocks // group_size, group_size, TOPN)

    def attend(operands):
        q_block, positions_in = operands
        gathered = jnp.take(tile_table, positions_in.reshape(-1), axis=0).reshape(
            group_size, TOPN * BLOCK, 2 * DH
        )
        scores = jnp.einsum(
            "gqd,gkd->gqk", q_block, gathered[..., :DH], preferred_element_type=jnp.float32
        ) * DH ** (-0.5)
        weights = jnp.exp(scores - jnp.max(scores, axis=-1, keepdims=True))
        totals = jnp.sum(weights, axis=-1, keepdims=True)
        weighted = jnp.einsum(
            "gqk,gkd->gqd",
            weights.astype(jnp.bfloat16),
            gathered[..., DH:],
            preferred_element_type=jnp.float32,
        )
        return (weighted / totals).astype(jnp.bfloat16)

    result = lax.map(attend, (q_groups, p_groups))
    return result.reshape(query_blocks * QB, H * DH)


def solution(mesh):
    placed = (
        P(("pb", "kv"), None),
        P(("kv", "pb"), None),
        P(("kv", "pb"), None),
        P(("pb", "kv"), None),
    )
    return jax.shard_map(
        per_device, mesh=mesh, in_specs=placed, out_specs=P(("pb", "kv"), None), check_vma=False
    )
```

profile of v0, /device:TPU:2, one launch (start us, length us, event | category | flops | bytes accessed | tf_op | source)
XLA Modules:
  0.0 519.4 jit_solution(11960891043452149832)
XLA Ops:
  6.5 2.3 pad_maximum_fusion.1
  9.0 0.1 add.105
  9.0 0.8 copy.30
  9.8 0.1 eq.45
  9.9 1.7 convert_reduce_fusion
  11.8 0.1 copy.38
  11.9 0.1 reshape.205
  12.1 13.5 %all_to_all.11 = s32[16,1,32]{2,1,0:T(1,128)S(1)} all-to-all(s32[16,1,32]{2,1,0:T(1,128)S(1)} %bitcast.44), channel_id=1, replica_groups=mesh['pb'=16,'kv'=16] {'kv'}, dimensions={0} | all-to-all | bytes 4096 | tf_op jit(solution)/shard_map/all_to_all | solution.py:50
  25.5 0.5 broadcast.157
  26.0 0.6 reduce.3
  26.7 80.8 %all-gather.2.cloned.1.call-done = bf16[512,64,256]{2,1,0:T(8,128)(2,1)} async-done(((bf16[32,64,256]{2,1,0:T(8,128)(2,1)}), bf16[512,64,256]{2,1,0:T(8,128)(2,1)}) %all-gather.2.cloned.1.call-update) | async-done | bytes 16777232 | tf_op jit(solution)/shard_map/all_gather | solution.py:39
  107.6 19.5 %gather_fusion.2 = bf16[512,64,256]{2,1,0:T(8,128)(2,1)} fusion(bf16[512,64,256]{2,1,0:T(8,128)(2,1)} %all-gather.2.cloned.1.call-done, s32[1024]{0:T(1024)S(1)} %pad_clamp_fusion.1), kind=kCustom, calls=%fused_computation.2 | custom fusion | bytes 33556480 | tf_op jit(solution)/shard_map/jit(_take)/gather | solution.py:51
  127.0 14.1 %broadcast_select_fusion = bf16[16,32,64,256]{3,2,1,0:T(8,128)(2,1)} fusion(bf16[16,32,64,256]{3,2,1,0:T(8,128)(2,1)} %bitcast.40, pred[16,32]{1,0:T(8,128)(4,1)S(1)} %compare_and_fusion.1), kind=kLoop, calls=%fused_computation.27 | loop fusion | flops 8388608 | bytes 33554944 | tf_op jit(solution)/shard_map/jit(_take)/select_n | solution.py:51
  141.2 7.4 %all-to-all-start.1 = ((bf16[16,32,64,256]{3,2,1,0:T(8,128)(2,1)}), bf16[16,32,64,256]{3,2,1,0:T(8,128)(2,1)}, u32[]{:S(2)}, u32[]{:S(2)}) async-start(bf16[16,32,64,256]{3,2,1,0:T(8,128)(2,1)} %broadcast_select_fusion), calls=%async_computation.1 | async-start | bytes 33554432 | tf_op jit(solution)/shard_map/all_to_all | solution.py:54
  148.6 0.1 copy.37
  148.8 0.1 reshape.222
  148.9 0.1 sub.27
  149.0 2.5 gather_fusion.1
  151.5 0.1 reshape.221
  151.6 0.1 pad_add_fusion
  151.7 0.8 fusion.23
  152.5 0.7 maximum_select_fusion
  153.3 4.1 reshape.203
  157.4 264.4 %all-reduce.2.cloned.1.call-done = bf16[2,64,256]{2,1,0:T(8,128)(2,1)} async-done(((bf16[2,64,256]{2,1,0:T(8,128)(2,1)}), bf16[2,64,256]{2,1,0:T(8,128)(2,1)}) %all-reduce.2.cloned.1.call-update) | async-done | bytes 65552 | tf_op jit(solution)/shard_map/psum | solution.py:63
  421.9 14.1 %pad_maximum_fusion = bf16[514,64,256]{2,1,0:T(8,128)(2,1)} fusion(bf16[2,64,256]{2,1,0:T(8,128)(2,1)} %all-reduce.2.cloned.1.call-done, bf16[512,64,256]{2,1,0:T(8,128)(2,1)} %bitcast.12), kind=kLoop, calls=%fused_computation.26 | loop fusion | flops 8421376 | bytes 33685504 | tf_op jit(solution)/shard_map/concatenate | solution.py:64
  436.0 70.9 %while.10 = (s32[]{:T(128)}, bf16[3,8,512,128]{3,2,1,0:T(8,128)(2,1)}, bf16[3,8,512,128]{3,2,1,0:T(8,128)(2,1)S(1)}, s32[3,8,16]{2,1,0:T(8,128)S(1)}, bf16[514,64,256]{2,1,0:T(8,128)(2,1)}, /*index=5*/s32[]{:T(128)}) while((s32[]{:T(128)}, bf16[3,8,512,128]{3,2,1,0:T(8,128)(2,1)}, bf16[3,8,512,128]{3,2,1,0:T(8,128)(2,1)S(1)}, ...), condition=%wide.region_7.8_spmd, body=%wide.region_4.7_spmd.sunk | while | flops 2184177664 | bytes 73523544 | solution.py:92
  436.1 0.1 broadcast_in_dim.101
  436.2 0.1 broadcast_in_dim.102
  436.3 8.5 %gather_fusion = bf16[128,64,256]{2,1,0:T(8,128)(2,1)} fusion(bf16[514,64,256]{2,1,0:T(8,128)(2,1)} %get-tuple-element.104, s32[1024]{0:T(1024)S(1)} %pad_clamp_fusion.4), kind=kCustom, calls=%fused_computation.clone.1 | custom fusion | bytes 8389120 | tf_op jit(solution)/shard_map/while/body/eval_jaxpr/jit(_take)/gather | solution.py:76
  444.8 4.6 bitcast_select_fusion.2
  449.4 2.4 multiply_reduce_fusion.2
  451.8 3.5 fusion.31
  455.3 4.2 bitcast_dynamic-update-slice_fusion.2
  459.7 0.1 broadcast_in_dim.101
  459.8 0.1 broadcast_in_dim.102
  459.9 8.5 %gather_fusion = bf16[128,64,256]{2,1,0:T(8,128)(2,1)} fusion(bf16[514,64,256]{2,1,0:T(8,128)(2,1)} %get-tuple-element.104, s32[1024]{0:T(1024)S(1)} %pad_clamp_fusion.4), kind=kCustom, calls=%fused_computation.clone.1 | custom fusion | bytes 8389120 | tf_op jit(solution)/shard_map/while/body/eval_jaxpr/jit(_take)/gather | solution.py:76
  468.4 4.6 bitcast_select_fusion.2
  473.0 2.4 multiply_reduce_fusion.2
  475.4 3.5 fusion.31
  479.0 4.2 bitcast_dynamic-update-slice_fusion.2
  483.3 0.1 broadcast_in_dim.101
  483.4 0.1 broadcast_in_dim.102
  483.5 8.5 %gather_fusion = bf16[128,64,256]{2,1,0:T(8,128)(2,1)} fusion(bf16[514,64,256]{2,1,0:T(8,128)(2,1)} %get-tuple-element.104, s32[1024]{0:T(1024)S(1)} %pad_clamp_fusion.4), kind=kCustom, calls=%fused_computation.clone.1 | custom fusion | bytes 8389120 | tf_op jit(solution)/shard_map/while/body/eval_jaxpr/jit(_take)/gather | solution.py:76
  492.0 4.6 bitcast_select_fusion.2
  496.6 2.4 multiply_reduce_fusion.2
  499.0 3.5 fusion.31
  502.6 4.2 bitcast_dynamic-update-slice_fusion.2
  506.8 5.8 %reshape.211 = bf16[1536,1024]{1,0:T(8,128)(2,1)} reshape(bf16[3,8,512,128]{3,2,1,0:T(8,128)(2,1)} %get-tuple-element.32) | data formatting | bytes 6291456 | tf_op jit(solution)/shard_map/reshape | solution.py:93
  (38 shorter events, 0.8 us)
Async XLA Ops:
  6.5 101.0 %all-gather.2.cloned.1.call-start = ((), (), s32[]{:S(2)}) async-start(), calls=%async_computation.2 | async-start | bytes 17825792 | tf_op jit(solution)/shard_map/all_gather | solution.py:39
  141.2 7.5 %copy-start = (s32[2]{0:T(128)S(1)}, s32[2]{0:T(128)}, u32[]{:S(2)}) copy-start(s32[2]{0:T(128)} %constant.100.clone) | copy-start | bytes 28
  141.2 280.7 %all-to-all-start.1 = ((bf16[16,32,64,256]{3,2,1,0:T(8,128)(2,1)}), bf16[16,32,64,256]{3,2,1,0:T(8,128)(2,1)}, u32[]{:S(2)}, u32[]{:S(2)}) async-start(bf16[16,32,64,256]{3,2,1,0:T(8,128)(2,1)} %broadcast_select_fusion), calls=%async_computation.1 | async-start | bytes 33554432 | tf_op jit(solution)/shard_map/all_to_all | solution.py:54
  148.6 273.3 %all-reduce.2.cloned.1.call-start = ((), (), s32[]{:S(2)}) async-start(), calls=%async_computation.3 | async-start | bytes 131072 | tf_op jit(solution)/shard_map/psum | solution.py:63
Sparse Core Ops, SparseCore 0:
  9.2 98.3 all-gather.1
  153.3 268.4 all-reduce.1
where the time goes:
time: 521 us; the launch traced here: 519 us
  waiting for transfers between devices  345 us (66%)
  local copies, waits for them, and re-layouts  61.3 us (12%)
  other arithmetic  58.3 us (11%)
  matrix products  20 us (4%)
  between operations  13.6 us (3%)
  blocking collectives  13.5 us (3%)
  starting transfers between devices  7.43 us (1%)
    psum x1, waiting for transfers between devices, per_device(): ends = lax.psum(ends, 'kv')  264 us
    all_gather x1, waiting for transfers between devices, per_device(): column = lax.all_gather(tiles_local, 'pb', axis=0, tiled=True)  80.8 us
    gather x3, local copies, waits for them, and re-layouts, attend(): jnp.take(tile_table, positions_in.reshape(-1), axis=0)  25.6 us
    gather x1, local copies, waits for them, and re-layouts, per_device(): jnp.take(column, asked_for.reshape(-1), axis=0)  19.5 us
    select_n x2, other arithmetic, per_device(): jnp.take(column, asked_for.reshape(-1), axis=0)  14.1 us
    concatenate x1, other arithmetic, per_device(): tile_table = jnp.concatenate([tile_table, ends], axis=0)  14.1 us
    select_n x6, other arithmetic, attend(): jnp.take(tile_table, positions_in.reshape(-1), axis=0)  13.7 us
    all_to_all x1, blocking collectives, per_device(): lax.all_to_all(by_column, 'kv', split_axis=0, concat_axis=0, tiled=True)  13.5 us
  transfers between devices with their start and end apart: 3, of which 2 were waited for; matrix products, arithmetic and copies ran while one was open for 3% of the time, Pallas kernels for 0%

commit v1 on v0

--- a/solution.py
+++ b/solution.py
@@ -60,7 +60,7 @@
     ends = jnp.where(
         jnp.stack([me_kv == 0, me_kv == kv_count - 1])[:, None, None], ends, jnp.zeros_like(ends)
     )
-    ends = lax.psum(ends, "kv")
+    ends = jnp.sum(lax.all_gather(ends, "kv"), axis=0)
     tile_table = jnp.concatenate([tile_table, ends], axis=0)
     extra_base = devices * slots
     leading_positions = jnp.broadcast_to(

time: 521 us -> 504 us (0.967); the launches traced: 519 us -> 496 us
  waiting for transfers between devices: 345 us -> 320 us
    psum x1 -> x0, waiting for transfers between devices: 264 us -> none  [per_device(): ends = lax.psum(ends, 'kv')]
    all_gather x0 -> x1, waiting for transfers between devices: none -> 221 us  [per_device(): ends = jnp.sum(lax.all_gather(ends, 'kv'), axis=0)]
    all_to_all x1, waiting for transfers between devices: 0.01 us -> 18.9 us  [per_device(): lax.all_to_all(outgoing, 'kv', split_axis=0, concat_axis=0, tiled=True)]
  transfers between devices with their start and end apart: 3 -> 3, of which waited for: 2 -> 3; matrix products, arithmetic and copies ran while one was open for 3% -> 3% of each run, Pallas kernels for 0% -> 0%
where the time goes in v1:
time: 504 us; the launch traced here: 496 us
  waiting for transfers between devices  320 us (63%)
  local copies, waits for them, and re-layouts  61.3 us (12%)
  other arithmetic  59.6 us (12%)
  matrix products  20 us (4%)
  between operations  13.6 us (3%)
  blocking collectives  13.5 us (3%)
  starting transfers between devices  7.43 us (1%)
    all_gather x1, waiting for transfers between devices, per_device(): ends = jnp.sum(lax.all_gather(ends, 'kv'), axis=0)  221 us
    all_gather x1, waiting for transfers between devices, per_device(): column = lax.all_gather(tiles_local, 'pb', axis=0, tiled=True)  80.8 us
    gather x3, local copies, waits for them, and re-layouts, attend(): jnp.take(tile_table, positions_in.reshape(-1), axis=0)  25.6 us
    gather x1, local copies, waits for them, and re-layouts, per_device(): jnp.take(column, asked_for.reshape(-1), axis=0)  19.5 us
    all_to_all x1, waiting for transfers between devices, per_device(): lax.all_to_all(outgoing, 'kv', split_axis=0, concat_axis=0, tiled=True)  18.9 us
    select_n x2, other arithmetic, per_device(): jnp.take(column, asked_for.reshape(-1), axis=0)  14.1 us
    concatenate x1, other arithmetic, per_device(): tile_table = jnp.concatenate([tile_table, ends], axis=0)  14 us
    select_n x6, other arithmetic, attend(): jnp.take(tile_table, positions_in.reshape(-1), axis=0)  13.7 us
  transfers between devices with their start and end apart: 3, of which 3 were waited for; matrix products, arithmetic and copies ran while one was open for 3% of the time, Pallas kernels for 0%

profile of v1, /device:TPU:2, one launch (start us, length us, event | category | flops | bytes accessed | tf_op | source)
XLA Modules:
  0.0 495.9 jit_solution(17721883774798702279)
XLA Ops:
  6.5 2.3 pad_maximum_fusion.1
  9.0 0.1 add.103
  9.0 0.8 copy.30
  9.8 0.1 eq.45
  9.9 1.7 convert_reduce_fusion
  11.8 0.1 copy.38
  11.9 0.1 reshape.234
  12.1 13.5 %all_to_all.11 = s32[16,1,32]{2,1,0:T(1,128)S(1)} all-to-all(s32[16,1,32]{2,1,0:T(1,128)S(1)} %bitcast.48), channel_id=1, replica_groups=mesh['pb'=16,'kv'=16] {'kv'}, dimensions={0} | all-to-all | bytes 4096 | tf_op jit(solution)/shard_map/all_to_all | solution.py:50
  25.5 0.5 broadcast.171
  26.0 0.6 reduce.4
  26.7 80.8 %all-gather.3.cloned.1.call-done = bf16[512,64,256]{2,1,0:T(8,128)(2,1)} async-done(((bf16[32,64,256]{2,1,0:T(8,128)(2,1)}), bf16[512,64,256]{2,1,0:T(8,128)(2,1)}) %all-gather.3.cloned.1.call-update) | async-done | bytes 16777232 | tf_op jit(solution)/shard_map/all_gather | solution.py:39
  107.6 19.5 %gather_fusion.2 = bf16[512,64,256]{2,1,0:T(8,128)(2,1)} fusion(bf16[512,64,256]{2,1,0:T(8,128)(2,1)} %all-gather.3.cloned.1.call-done, s32[1024]{0:T(1024)S(1)} %pad_clamp_fusion.1), kind=kCustom, calls=%fused_computation.2 | custom fusion | bytes 33556480 | tf_op jit(solution)/shard_map/jit(_take)/gather | solution.py:51
  127.0 14.1 %broadcast_select_fusion = bf16[16,32,64,256]{3,2,1,0:T(8,128)(2,1)} fusion(bf16[16,32,64,256]{3,2,1,0:T(8,128)(2,1)} %bitcast.44, pred[16,32]{1,0:T(8,128)(4,1)S(1)} %compare_and_fusion.1), kind=kLoop, calls=%fused_computation.27 | loop fusion | flops 8388608 | bytes 33554944 | tf_op jit(solution)/shard_map/jit(_take)/select_n | solution.py:51
  141.2 7.4 %all-to-all-start.1 = ((bf16[16,32,64,256]{3,2,1,0:T(8,128)(2,1)}), bf16[16,32,64,256]{3,2,1,0:T(8,128)(2,1)}, u32[]{:S(2)}, u32[]{:S(2)}) async-start(bf16[16,32,64,256]{3,2,1,0:T(8,128)(2,1)} %broadcast_select_fusion), calls=%async_computation.1 | async-start | bytes 33554432 | tf_op jit(solution)/shard_map/all_to_all | solution.py:54
  148.7 0.8 slice_bitcast_fusion.1
  149.5 0.7 maximum_select_fusion
  150.2 0.1 copy.37
  150.4 0.1 reshape.251
  150.4 0.1 sub.27
  150.6 2.5 gather_fusion.1
  153.1 0.1 reshape.250
  153.2 4.1 reshape.232
  157.4 220.7 %all-gather.5.cloned.1.call-done = bf16[16,2,64,256]{3,2,1,0:T(8,128)(2,1)} async-done(((bf16[1,2,64,256]{3,2,1,0:T(8,128)(2,1)}), bf16[16,2,64,256]{3,2,1,0:T(8,128)(2,1)}) %all-gather.5.cloned.1.call-update) | async-done | bytes 1048592 | tf_op jit(solution)/shard_map/all_gather | solution.py:63
  378.2 1.4 reduce_sum.31
  379.5 18.9 %all-to-all-done.1 = bf16[16,32,64,256]{3,2,1,0:T(8,128)(2,1)} async-done(((bf16[16,32,64,256]{3,2,1,0:T(8,128)(2,1)}), bf16[16,32,64,256]{3,2,1,0:T(8,128)(2,1)}, u32[]{:S(2)}, u32[]{:S(2)}) %all-to-all-start.1) | async-done | bytes 16777248 | tf_op jit(solution)/shard_map/all_to_all | solution.py:54
  398.4 14.0 %pad_maximum_fusion = bf16[514,64,256]{2,1,0:T(8,128)(2,1)} fusion(bf16[2,64,256]{2,1,0:T(8,128)(2,1)S(1)} %reduce_sum.31, bf16[512,64,256]{2,1,0:T(8,128)(2,1)} %bitcast.12), kind=kLoop, calls=%fused_computation.26 | loop fusion | flops 8421376 | bytes 33685504 | tf_op jit(solution)/shard_map/concatenate | solution.py:64
  412.4 70.9 %while.10 = (s32[]{:T(128)}, bf16[3,8,512,128]{3,2,1,0:T(8,128)(2,1)}, bf16[3,8,512,128]{3,2,1,0:T(8,128)(2,1)S(1)}, s32[3,8,16]{2,1,0:T(8,128)S(1)}, bf16[514,64,256]{2,1,0:T(8,128)(2,1)}, /*index=5*/s32[]{:T(128)}) while((s32[]{:T(128)}, bf16[3,8,512,128]{3,2,1,0:T(8,128)(2,1)}, bf16[3,8,512,128]{3,2,1,0:T(8,128)(2,1)S(1)}, ...), condition=%wide.region_7.8_spmd, body=%wide.region_4.7_spmd.sunk | while | flops 2184177664 | bytes 73523544 | solution.py:92
  412.6 0.1 broadcast_in_dim.102
  412.7 8.5 %gather_fusion = bf16[128,64,256]{2,1,0:T(8,128)(2,1)} fusion(bf16[514,64,256]{2,1,0:T(8,128)(2,1)} %get-tuple-element.104, s32[1024]{0:T(1024)S(1)} %pad_clamp_fusion.4), kind=kCustom, calls=%fused_computation.clone.1 | custom fusion | bytes 8389120 | tf_op jit(solution)/shard_map/while/body/eval_jaxpr/jit(_take)/gather | solution.py:76
  421.3 4.6 bitcast_select_fusion.2
  425.8 2.4 multiply_reduce_fusion.2
  428.3 3.5 fusion.30
  431.8 4.2 bitcast_dynamic-update-slice_fusion.2
  436.2 0.1 broadcast_in_dim.101
  436.2 0.1 broadcast_in_dim.102
  436.3 8.5 %gather_fusion = bf16[128,64,256]{2,1,0:T(8,128)(2,1)} fusion(bf16[514,64,256]{2,1,0:T(8,128)(2,1)} %get-tuple-element.104, s32[1024]{0:T(1024)S(1)} %pad_clamp_fusion.4), kind=kCustom, calls=%fused_computation.clone.1 | custom fusion | bytes 8389120 | tf_op jit(solution)/shard_map/while/body/eval_jaxpr/jit(_take)/gather | solution.py:76
  444.9 4.6 bitcast_select_fusion.2
  449.5 2.4 multiply_reduce_fusion.2
  451.9 3.5 fusion.30
  455.4 4.2 bitcast_dynamic-update-slice_fusion.2
  459.8 0.1 broadcast_in_dim.101
  459.9 0.1 broadcast_in_dim.102
  460.0 8.5 %gather_fusion = bf16[128,64,256]{2,1,0:T(8,128)(2,1)} fusion(bf16[514,64,256]{2,1,0:T(8,128)(2,1)} %get-tuple-element.104, s32[1024]{0:T(1024)S(1)} %pad_clamp_fusion.4), kind=kCustom, calls=%fused_computation.clone.1 | custom fusion | bytes 8389120 | tf_op jit(solution)/shard_map/while/body/eval_jaxpr/jit(_take)/gather | solution.py:76
  468.5 4.6 bitcast_select_fusion.2
  473.1 2.4 multiply_reduce_fusion.2
  475.5 3.5 fusion.30
  479.0 4.2 bitcast_dynamic-update-slice_fusion.2
  483.3 5.8 %reshape.240 = bf16[1536,1024]{1,0:T(8,128)(2,1)} reshape(bf16[3,8,512,128]{3,2,1,0:T(8,128)(2,1)} %get-tuple-element.32) | data formatting | bytes 6291456 | tf_op jit(solution)/shard_map/reshape | solution.py:93
  (39 shorter events, 0.9 us)
Async XLA Ops:
  6.5 101.0 %all-gather.3.cloned.1.call-start = ((), (), s32[]{:S(2)}) async-start(), calls=%async_computation.2 | async-start | bytes 17825792 | tf_op jit(solution)/shard_map/all_gather | solution.py:39
  141.2 9.1 %copy-start = (s32[2]{0:T(128)S(1)}, s32[2]{0:T(128)}, u32[]{:S(2)}) copy-start(s32[2]{0:T(128)} %constant.102.clone) | copy-start | bytes 28
  141.2 257.2 %all-to-all-start.1 = ((bf16[16,32,64,256]{3,2,1,0:T(8,128)(2,1)}), bf16[16,32,64,256]{3,2,1,0:T(8,128)(2,1)}, u32[]{:S(2)}, u32[]{:S(2)}) async-start(bf16[16,32,64,256]{3,2,1,0:T(8,128)(2,1)} %broadcast_select_fusion), calls=%async_computation.1 | async-start | bytes 33554432 | tf_op jit(solution)/shard_map/all_to_all | solution.py:54
  148.6 229.6 %all-gather.5.cloned.1.call-start = ((), (), s32[]{:S(2)}) async-start(), calls=%async_computation.3 | async-start | bytes 1114112 | tf_op jit(solution)/shard_map/all_gather | solution.py:63
Sparse Core Ops, SparseCore 0:
  9.2 98.3 all-gather.2
  151.8 226.2 all-gather.4
